TPU v7x, 512 devices: a whole 4x4x16 slice. The times are simulated.
512 devices in a mesh: row: 64 (over z, x_hi, core), rep: 8 (over y, x_lo).
Axes of the slice: x: 4 (x_hi: 2, x_lo: 2; x = x_hi * 2 + x_lo), y: 4, z: 16, core: 2. Of those that a mesh axis runs over, the one named last changes fastest.
Arguments:
- features: float32 [65536, 128], P(('row', 'rep')), may hold values from -6 to 6
- weight: float32 [128, 256], replicated, may hold values from -0.5 to 0.5
- bias: float32 [256], replicated, may hold values from -3 to 3
- adjacency: float32 [64, 8, 64, 128, 128], P('row', 'rep')
- tile_row: int32 [64, 8, 64], P('row', 'rep'), may hold values from 0 to 7
- tile_live: int32 [64, 8, 64], P('row', 'rep'), may hold values from 0 to 1
- node_live: int32 [65536], P(('row', 'rep')), may hold values 0 or 1
- cotangent: float32 [65536, 256], P(('row', 'rep'))
Outputs:
- activations: float32 [65536, 256], P(('row', 'rep'))
- weight_grad: float32 [128, 256], replicated
- bias_grad: float32 [256], replicated
All inputs are finite; a program needn't handle non-finite values. No bound on the sum of `node_live` on one device may be relied on, other than what follows from the above.
Results may differ from a plain program's by a relative error of at most 0.0003.
Values sent between devices are 32-bit elements; how exact they have to be, the bound alone decides.
A program may use at most 64 MiB of HBM per device.

v0:
```python
import jax
import jax.numpy as jnp
from jax import lax
from jax.sharding import PartitionSpec as P


def section_terms(adj_tiles, row_slot, live_slot, pieces, totals):
    tile_size = adj_tiles.shape[1]
    piece_rows = pieces[0].shape[0]
    shard_count = piece_rows // tile_size

    def add_tile(k, sums_in):
        tile_now = lax.dynamic_index_in_dim(adj_tiles, k, 0, keepdims=False)
        target = lax.dynamic_index_in_dim(row_slot, k, 0, keepdims=False) * tile_size
        weight_now = lax.dynamic_index_in_dim(live_slot, k, 0, keepdims=False)
        updated = []
        for piece_now, total in zip(pieces, sums_in):
            feat_block = lax.dynamic_slice_in_dim(piece_now, k * tile_size, tile_size, 0)
            tile_term = jnp.dot(tile_now, feat_block, precision=lax.Precision.HIGHEST) * weight_now
            current = lax.dynamic_slice_in_dim(total, target, tile_size, 0)
            updated.append(lax.dynamic_update_slice_in_dim(total, current + tile_term, target, 0))
        return tuple(updated)

    return lax.fori_loop(0, shard_count, add_tile, tuple(totals))


def local(features, weight, bias, adjacency, tile_row, tile_live, node_live, cotangent):
    adj_tiles = adjacency[0, 0]
    row_slot = tile_row[0, 0]
    live_slot = tile_live[0, 0].astype(jnp.float32)
    groups = lax.axis_size("rep")
    tile_size = adj_tiles.shape[1]
    empty_in = jnp.zeros((groups * tile_size, features.shape[1]), jnp.float32)
    partial_in = section_terms(
        adj_tiles,
        row_slot,
        live_slot,
        (lax.all_gather(features, "row", axis=0, tiled=True),),
        (empty_in,),
    )[0]
    aggregated = lax.psum_scatter(partial_in, "rep", scatter_dimension=0, tiled=True)
    projected_sum = jnp.dot(aggregated, weight, precision=lax.Precision.HIGHEST)
    preact = projected_sum + bias
    node_mask = node_live.astype(jnp.float32)[:, None]
    sigmoid_value = jax.nn.sigmoid(preact)
    activations = preact * sigmoid_value * node_mask
    local_grad = cotangent * node_mask * sigmoid_value * (1.0 + preact * (1.0 - sigmoid_value))
    weight_part = lax.dot_general(
        aggregated, local_grad, (((0,), (0,)), ((), ())), precision=lax.Precision.HIGHEST
    )
    bias_part = jnp.sum(local_grad, axis=0)
    weight_grad, bias_grad = lax.psum((weight_part, bias_part), ("row", "rep"))
    return (activations, weight_grad, bias_grad)


def solution(mesh):
    placed = (
        P(("row", "rep"), None),
        P(),
        P(),
        P("row", "rep", None, None, None),
        P("row", "rep", None),
        P("row", "rep", None),
        P(("row", "rep")),
        P(("row", "rep"), None),
    )
    return jax.shard_map(
        local,
        mesh=mesh,
        in_specs=placed,
        out_specs=(P(("row", "rep"), None), P(), P()),
        check_vma=False,
    )
```

profile of v0, /device:TPU:1, one launch (start us, length us, event | category | flops | bytes accessed | tf_op | source)
XLA Modules:
  0.0 943.0 jit_solution(5304687563539046468)
XLA Ops:
  8.6 159.4 %all-gather.2.cloned.1.call-done = f32[8192,128]{1,0:T(8,128)} async-done(((f32[128,128]{1,0:T(8,128)}), f32[8192,128]{1,0:T(8,128)}) %all-gather.2.cloned.1.call-update) | async-done | bytes 4194320 | tf_op jit(solution)/shard_map/all_gather | solution.py:38
  168.1 271.4 %while.13 = (s32[]{:T(128)}, f32[1024,128]{1,0:T(8,128)S(1)}, s32[64]{0:T(128)}, f32[64,128,128]{2,1,0:T(8,128)}, f32[8192,128]{1,0:T(8,128)}, /*index=5*/f32[64...) while((s32[]{:T(128)}, f32[1024,128]{1,0:T(8,128)S(1)}, ...), condition=%wide.region_1.2_spmd, body=%wide.region_0.1_spmd.sunk | while | flops 25198600 | bytes 263409 | solution.py:24
  170.6 1.7 fusion.17
  174.9 1.7 fusion.17
  179.1 1.7 fusion.17
  183.3 1.7 fusion.17
  187.6 1.7 fusion.17
  191.8 1.7 fusion.17
  196.1 1.7 fusion.17
  200.3 1.7 fusion.17
  208.8 1.7 fusion.17
  221.5 1.7 fusion.17
  225.7 1.7 fusion.17
  230.0 1.7 fusion.17
  234.2 1.7 fusion.17
  242.7 1.7 fusion.17
  255.4 1.7 fusion.17
  263.9 1.7 fusion.17
  268.2 1.7 fusion.17
  276.6 1.7 fusion.17
  285.1 1.7 fusion.17
  289.4 1.7 fusion.17
  297.8 1.7 fusion.17
  302.1 1.7 fusion.17
  310.6 1.7 fusion.17
  319.0 1.7 fusion.17
  323.3 1.7 fusion.17
  331.8 1.7 fusion.17
  336.0 1.7 fusion.17
  344.5 1.7 fusion.17
  353.0 1.7 fusion.17
  357.2 1.7 fusion.17
  365.7 1.7 fusion.17
  369.9 1.7 fusion.17
  378.4 1.7 fusion.17
  386.9 1.7 fusion.17
  391.1 1.7 fusion.17
  399.6 1.7 fusion.17
  403.9 1.7 fusion.17
  412.4 1.7 fusion.17
  425.1 1.7 fusion.17
  433.6 1.7 fusion.17
  437.8 1.7 fusion.17
  441.1 34.6 %reduce-scatter.2.cloned.1.call-done = f32[128,128]{1,0:T(8,128)} async-done(((f32[1024,128]{1,0:T(8,128)}), f32[128,128]{1,0:T(8,128)}) %reduce-scatter.2.cloned.1.call-update) | async-done | bytes 65552 | tf_op jit(solution)/shard_map/reduce_scatter | solution.py:41
  475.7 1.9 fusion.6
  477.5 1.8 fusion.7
  479.4 106.9 %psum.15 = f32[256]{0:T(256)} all-reduce(f32[256]{0:T(256)S(1)} %get-tuple-element.125), channel_id=1, replica_groups=mesh['row'=64,'rep'=8] {'row','rep'}, use_global_device_ids=true, to_apply=%region_5.6 | all-reduce | flops 256 | bytes 2048 | tf_op jit(solution)/shard_map/psum | solution.py:52
  586.3 348.6 %all-reduce.2.cloned.1.call-done = f32[128,256]{1,0:T(8,128)} async-done(((f32[128,256]{1,0:T(8,128)}), f32[128,256]{1,0:T(8,128)}) %all-reduce.2.cloned.1.call-update) | async-done | bytes 131088 | tf_op jit(solution)/shard_map/psum | solution.py:52
  (165 shorter events, 161.2 us)
Async XLA Ops:
  7.2 468.5 %copy-start = (f32[128,256]{1,0:T(8,128)S(1)}, f32[128,256]{1,0:T(8,128)}, u32[]{:S(2)}) copy-start(f32[128,256]{1,0:T(8,128)} %param.11) | copy-start | bytes 393220
  7.2 160.9 %all-gather.2.cloned.1.call-start = ((), (), s32[]{:S(2)}) async-start(), calls=%async_computation.1 | async-start | bytes 4259840 | tf_op jit(solution)/shard_map/all_gather | solution.py:38
  7.9 467.7 %reduce-scatter.2.cloned.1.call-start = ((), (), s32[]{:S(2)}) async-start(), calls=%async_computation.2 | async-start | bytes 589824 | tf_op jit(solution)/shard_map/reduce_scatter | solution.py:41
  439.5 0.8 copy-start.1
  440.3 494.6 %all-reduce.2.cloned.1.call-start = ((), (), s32[]{:S(2)}) async-start(), calls=%async_computation.3 | async-start | bytes 262144 | tf_op jit(solution)/shard_map/psum | solution.py:52
Sparse Core Ops, SparseCore 0:
  11.3 156.7 all-gather.1
  440.5 35.1 reduce-scatter.1
  482.6 452.2 all-reduce.1
where the time goes:
time: 948 us; the launch traced here: 943 us
  waiting for transfers between devices  543 us (57%)
  local copies, waits for them, and re-layouts  119 us (13%)
  matrix products  114 us (12%)
  blocking collectives  107 us (11%)
  loops' own time  44.1 us (5%)
  between operations  13.8 us (1%)
    psum x1, waiting for transfers between devices, local(): weight_grad, bias_grad = lax.psum((weight_part, bias_part), ('row', 'rep'))  349 us
    all_gather x1, waiting for transfers between devices, local(): lax.all_gather(features, 'row', axis=0, tiled=True)  159 us
    dot_general x64, matrix products, add_tile(): jnp.dot(tile_now, feat_block, precision=lax.Precision.HIGHEST) * weight_now  110 us
    psum x1, blocking collectives, local(): weight_grad, bias_grad = lax.psum((weight_part, bias_part), ('row', 'rep'))  107 us
    dynamic_slice x64, local copies, waits for them, and re-layouts, add_tile(): lax.dynamic_index_in_dim(row_slot, k, 0, keepdims=False) * tile_size  79.5 us
    another operation x1, loops' own time, section_terms(): return lax.fori_loop(0, shard_count, add_tile, tuple(totals))  44.1 us
    dynamic_slice x64, local copies, waits for them, and re-layouts, add_tile(): weight_now = lax.dynamic_index_in_dim(live_slot, k, 0, keepdims=False)  37.5 us
    reduce_scatter x1, waiting for transfers between devices, local(): lax.psum_scatter(partial_in, 'rep', scatter_dimension=0, tiled=True)  34.6 us
  transfers between devices with their start and end apart: 3, of which 3 were waited for; matrix products, arithmetic and copies ran while one was open for 0% of the time, Pallas kernels for 0%

commit v1 on v0

--- a/solution.py
+++ b/solution.py
@@ -49,7 +49,7 @@
         aggregated, local_grad, (((0,), (0,)), ((), ())), precision=lax.Precision.HIGHEST
     )
     bias_part = jnp.sum(local_grad, axis=0)
-    weight_grad, bias_grad = lax.psum((weight_part, bias_part), ("row", "rep"))
+    weight_grad, bias_grad = lax.psum(lax.psum((weight_part, bias_part), "rep"), "row")
     return (activations, weight_grad, bias_grad)
 
 

time: 948 us -> 1050 us (1.11)
  waiting for transfers between devices: 543 us -> 599 us
  blocking collectives: 107 us -> 153 us
    psum x1 -> x2, waiting for transfers between devices: 349 us -> 404 us  [the longest x1 317 us: local(): lax.psum(lax.psum((weight_part, bias_part), 'rep'), 'row')]
    psum x1 -> x2, blocking collectives: 107 us -> 153 us  [the longest x1 139 us: local(): lax.psum(lax.psum((weight_part, bias_part), 'rep'), 'row')]
  transfers between devices with their start and end apart: 3 -> 4, of which waited for: 3 -> 4; matrix products, arithmetic and copies ran while one was open for 0% -> 0% of each run, Pallas kernels for 0% -> 0%
where the time goes in v1:
time: 1050 us; the launch traced here: 1040 us
  waiting for transfers between devices  599 us (57%)
  blocking collectives  153 us (15%)
  local copies, waits for them, and re-layouts  119 us (11%)
  matrix products  114 us (11%)
  loops' own time  44.1 us (4%)
  between operations  13.8 us (1%)
    psum x1, waiting for transfers between devices, local(): lax.psum(lax.psum((weight_part, bias_part), 'rep'), 'row')  317 us
    all_gather x1, waiting for transfers between devices, local(): lax.all_gather(features, 'row', axis=0, tiled=True)  160 us
    psum x1, blocking collectives, local(): lax.psum(lax.psum((weight_part, bias_part), 'rep'), 'row')  139 us
    dot_general x64, matrix products, add_tile(): jnp.dot(tile_now, feat_block, precision=lax.Precision.HIGHEST) * weight_now  110 us
    psum x1, waiting for transfers between devices, local(): lax.psum((weight_part, bias_part), 'rep')  87.1 us
    dynamic_slice x64, local copies, waits for them, and re-layouts, add_tile(): lax.dynamic_index_in_dim(row_slot, k, 0, keepdims=False) * tile_size  79.5 us
    another operation x1, loops' own time, section_terms(): return lax.fori_loop(0, shard_count, add_tile, tuple(totals))  44.1 us
    dynamic_slice x64, local copies, waits for them, and re-layouts, add_tile(): weight_now = lax.dynamic_index_in_dim(live_slot, k, 0, keepdims=False)  37.5 us
  transfers between devices with their start and end apart: 4, of which 4 were waited for; matrix products, arithmetic and copies ran while one was open for 0% of the time, Pallas kernels for 0%

profile of v1, /device:TPU:1, one launch (start us, length us, event | category | flops | bytes accessed | tf_op | source)
XLA Modules:
  0.0 1044.1 jit_solution(5298063953844900420)
XLA Ops:
  8.6 159.5 %all-gather.2.cloned.1.call-done = f32[8192,128]{1,0:T(8,128)} async-done(((f32[128,128]{1,0:T(8,128)}), f32[8192,128]{1,0:T(8,128)}) %all-gather.2.cloned.1.call-update) | async-done | bytes 4194320 | tf_op jit(solution)/shard_map/all_gather | solution.py:38
  168.2 271.4 %while.13 = (s32[]{:T(128)}, f32[1024,128]{1,0:T(8,128)S(1)}, s32[64]{0:T(128)}, f32[64,128,128]{2,1,0:T(8,128)}, f32[8192,128]{1,0:T(8,128)}, /*index=5*/f32[64...) while((s32[]{:T(128)}, f32[1024,128]{1,0:T(8,128)S(1)}, ...), condition=%wide.region_1.2_spmd, body=%wide.region_0.1_spmd.sunk | while | flops 25198600 | bytes 263409 | solution.py:24
  170.7 1.7 fusion.17
  174.9 1.7 fusion.17
  179.2 1.7 fusion.17
  183.4 1.7 fusion.17
  191.9 1.7 fusion.17
  196.1 1.7 fusion.17
  204.6 1.7 fusion.17
  208.8 1.7 fusion.17
  217.3 1.7 fusion.17
  221.6 1.7 fusion.17
  230.1 1.7 fusion.17
  238.5 1.7 fusion.17
  242.8 1.7 fusion.17
  251.3 1.7 fusion.17
  255.5 1.7 fusion.17
  264.0 1.7 fusion.17
  272.5 1.7 fusion.17
  276.7 1.7 fusion.17
  285.2 1.7 fusion.17
  289.4 1.7 fusion.17
  297.9 1.7 fusion.17
  306.4 1.7 fusion.17
  310.6 1.7 fusion.17
  319.1 1.7 fusion.17
  323.4 1.7 fusion.17
  331.8 1.7 fusion.17
  340.3 1.7 fusion.17
  344.6 1.7 fusion.17
  353.0 1.7 fusion.17
  365.8 1.7 fusion.17
  374.2 1.7 fusion.17
  378.5 1.7 fusion.17
  382.7 1.7 fusion.17
  387.0 1.7 fusion.17
  399.7 1.7 fusion.17
  408.2 1.7 fusion.17
  412.4 1.7 fusion.17
  420.9 1.7 fusion.17
  433.6 1.7 fusion.17
  441.1 34.7 %reduce-scatter.2.cloned.1.call-done = f32[128,128]{1,0:T(8,128)} async-done(((f32[1024,128]{1,0:T(8,128)}), f32[128,128]{1,0:T(8,128)}) %reduce-scatter.2.cloned.1.call-update) | async-done | bytes 65552 | tf_op jit(solution)/shard_map/reduce_scatter | solution.py:41
  475.8 1.9 fusion.6
  477.7 1.8 fusion.7
  479.5 87.1 %all-reduce.3.cloned.1.call-done = f32[128,256]{1,0:T(8,128)} async-done(((f32[128,256]{1,0:T(8,128)}), f32[128,256]{1,0:T(8,128)}) %all-reduce.3.cloned.1.call-update) | async-done | bytes 131088 | tf_op jit(solution)/shard_map/psum | solution.py:52
  566.6 14.0 %psum.30 = f32[256]{0:T(256)S(1)} all-reduce(f32[256]{0:T(256)S(1)} %get-tuple-element.125), channel_id=1, replica_groups=mesh['row'=64,'rep'=8] {'rep'}, use_global_device_ids=true, to_apply=%region_6.7 | all-reduce | flops 256 | bytes 2048 | tf_op jit(solution)/shard_map/psum | solution.py:52
  580.7 138.8 %psum.31 = f32[256]{0:T(256)} all-reduce(f32[256]{0:T(256)S(1)} %psum.30), channel_id=1, replica_groups=mesh['row'=64,'rep'=8] {'row'}, use_global_device_ids=true, to_apply=%region_7.8 | all-reduce | flops 256 | bytes 2048 | tf_op jit(solution)/shard_map/psum | solution.py:52
  719.5 316.6 %all-reduce.5.cloned.1.call-done = f32[128,256]{1,0:T(8,128)} async-done(((f32[128,256]{1,0:T(8,128)}), f32[128,256]{1,0:T(8,128)}) %all-reduce.5.cloned.1.call-update) | async-done | bytes 131088 | tf_op jit(solution)/shard_map/psum | solution.py:52
  (169 shorter events, 164.7 us)
Async XLA Ops:
  7.2 468.6 %copy-start = (f32[128,256]{1,0:T(8,128)S(1)}, f32[128,256]{1,0:T(8,128)}, u32[]{:S(2)}) copy-start(f32[128,256]{1,0:T(8,128)} %param.11) | copy-start | bytes 393220
  7.2 161.0 %all-gather.2.cloned.1.call-start = ((), (), s32[]{:S(2)}) async-start(), calls=%async_computation.1 | async-start | bytes 4259840 | tf_op jit(solution)/shard_map/all_gather | solution.py:38
  7.9 467.9 %reduce-scatter.2.cloned.1.call-start = ((), (), s32[]{:S(2)}) async-start(), calls=%async_computation.2 | async-start | bytes 589824 | tf_op jit(solution)/shard_map/reduce_scatter | solution.py:41
  439.6 0.8 copy-start.1
  440.4 126.2 %all-reduce.3.cloned.1.call-start = ((), (), s32[]{:S(2)}) async-start(), calls=%async_computation.3 | async-start | bytes 262144 | tf_op jit(solution)/shard_map/psum | solution.py:52
  479.5 556.6 %all-reduce.5.cloned.1.call-start = ((), (), s32[]{:S(2)}) async-start(), calls=%async_computation.4 | async-start | bytes 262144 | tf_op jit(solution)/shard_map/psum | solution.py:52
Sparse Core Ops, SparseCore 0:
  11.3 156.7 all-gather.1
  440.5 35.2 reduce-scatter.1
  479.6 86.9 all-reduce.2
  569.4 466.6 all-reduce.4
